TPU v7x, 128 devices: a whole 4x4x4 slice. The times are simulated.
128 devices in a mesh: fx: 16 (over x, z), fy: 8 (over y, core).
Axes of the slice: x: 4, y: 4, z: 4, core: 2. Of those that a mesh axis runs over, the one named last changes fastest.
Arguments:
- fluid_state: float32 [5, 8, 2048, 1024], P(None, None, 'fx', 'fy'), may hold values from -0.3 to 2.8, as said below
- surface_points: float32 [16384, 3, 128], P(('fx', 'fy')), may hold values from 0 to 1
- surface_normals: float32 [16384, 3, 128], P(('fx', 'fy')), may hold values from -1 to 1
- owner_ids: int32 [16384, 1], P(('fx', 'fy')), may hold values from 0 to 127; in each aligned block of 128 rows (0 to 127, 128 to 255, ...) at most 2 rows name the same one
- support_ids: int32 [16384, 2], P(('fx', 'fy')), may hold values from 0 to 7
- struct_points: float32 [1024, 3, 128], P(('fx', 'fy')), may hold values from 0 to 1
- couplings: float32 [1024, 4, 128, 128], P(('fx', 'fy')), may hold values from 0.5 to 1
- coupling_pattern: int32 [1024, 4], P(('fx', 'fy')), may hold values from 0 to 7, as said below
- stiff_diagonal: float32 [1024, 128], P(('fx', 'fy')), may hold values from 1.05 to 1.6
- struct_load: float32 [1024, 3, 128], P(('fx', 'fy')), may hold values from -6 to 6
- predicted: float32 [1024, 3, 128], P(('fx', 'fy')), may hold values from -3 to 3
- hist_residual: float32 [8, 1024, 3, 128], P(None, ('fx', 'fy')), may hold values from -0.03 to 0.03
- hist_response: float32 [8, 1024, 3, 128], P(None, ('fx', 'fy')), may hold values from -6 to 6
Outputs:
- new_state: float32 [5, 8, 2048, 1024], P(None, None, 'fx', 'fy')
- next_estimate: float32 [1024, 3, 128], P(('fx', 'fy'))
- coupling_residual: float32 [1024, 3, 128], P(('fx', 'fy'))
Inputs may be any that keep to these rules, and one draw needn't show every extreme that they name: `fluid_state`: component 0 (density) lies in [0.8, 1.2], components 1 to 3 (momenta) in [-0.3, 0.3], component 4 (total energy) in [2.2, 2.8]. `owner_ids`: among the 128 surface blocks of one device (aligned blocks of rows), no owner is named by more than 2 of them. `support_ids`: local block numbers on the owner. For each device's 8 structure blocks and each column k, the entries coupling_pattern[., k] are a permutation of 0 to 7.
All inputs are finite; a program needn't handle non-finite values.
Results may differ from a plain program's by a relative error of at most 0.0003.
Values sent between devices are 32-bit elements; how exact they have to be, the bound alone decides.
No kernel may reach another device: no remote copies, remote signals or barrier semaphores. Data moves between devices by JAX's collectives and lax.ppermute only.
A program may use at most 192 MiB of HBM per device.

v0:
```python
import math
import jax
import jax.numpy as jnp
from jax import lax
from jax.sharding import PartitionSpec as P

CG_ITERS = 2
COUPLE = 2
TOP_PRECISION = lax.Precision.HIGHEST
STEP_RATIO = 0.12
WALL_SPEED = 0.5
WALL_GAIN = 0.5
LOAD_SCALE = 4.0
PRESSURE_REF = 0.98
RADIUS = 1.0


def with_halo(cells, sides, width):
    for axis, dim in sides:
        count = lax.axis_size(axis)
        head = lax.slice_in_dim(cells, 0, width, axis=dim)
        tail = lax.slice_in_dim(cells, cells.shape[dim] - width, cells.shape[dim], axis=dim)
        cells = jnp.concatenate(
            [
                lax.ppermute(tail, axis, [(i, (i + 1) % count) for i in range(count)]),
                cells,
                lax.ppermute(head, axis, [((i + 1) % count, i) for i in range(count)]),
            ],
            axis=dim,
        )
    return cells


def state_pressure(state):
    return 0.4 * (
        state[4]
        - 0.5 * (state[1] * state[1] + state[2] * state[2] + state[3] * state[3]) / state[0]
    )


def face_terms(state, momentum):
    density = state[0]
    velocity = state[momentum] / density
    pressure = state_pressure(state)
    flux = state * velocity
    flux = flux.at[momentum].add(pressure)
    flux = flux.at[4].add(pressure * velocity)
    speed = jnp.abs(velocity) + jnp.sqrt(1.4 * pressure / density)
    return (flux, speed)


def rusanov(left, right, left_flux, right_flux, left_speed, right_speed):
    return 0.5 * (left_flux + right_flux) - 0.5 * jnp.maximum(left_speed, right_speed) * (
        right - left
    )


def vertical_terms(state, wall):
    bottom = state[:, 0]
    ghost = bottom.at[3].set(2.0 * bottom[0] * wall - bottom[3])
    column = jnp.concatenate([ghost[:, None], state, state[:, -1:]], axis=1)
    flux, speed = face_terms(column, 3)
    faces = rusanov(column[:, :-1], column[:, 1:], flux[:, :-1], flux[:, 1:], speed[:-1], speed[1:])
    return faces[:, 1:] - faces[:, :-1]


def horizontal_terms(state):
    extended = with_halo(state, (("fx", 2), ("fy", 3)), 1)
    strip = extended[:, :, :, 1:-1]
    flux, speed = face_terms(strip, 1)
    faces = rusanov(
        strip[:, :, :-1],
        strip[:, :, 1:],
        flux[:, :, :-1],
        flux[:, :, 1:],
        speed[:, :-1],
        speed[:, 1:],
    )
    total = faces[:, :, 1:] - faces[:, :, :-1]
    strip = extended[:, :, 1:-1, :]
    flux, speed = face_terms(strip, 2)
    faces = rusanov(
        strip[:, :, :, :-1],
        strip[:, :, :, 1:],
        flux[:, :, :, :-1],
        flux[:, :, :, 1:],
        speed[:, :, :-1],
        speed[:, :, 1:],
    )
    return total + (faces[:, :, :, 1:] - faces[:, :, :, :-1])


def kernel_block(fluid_points, struct_nodes):
    squared = jnp.zeros((), jnp.float32)
    for axis in range(3):
        offset = fluid_points[..., axis, :, None] - struct_nodes[..., axis, None, :]
        squared = squared + offset * offset
    ratio = jnp.sqrt(squared) / RADIUS
    reach = jnp.maximum(1.0 - ratio, 0.0)
    return reach * reach * reach * reach * (4.0 * ratio + 1.0)


def owner_kernels(places, support, struct_points):
    rows = places.shape[0]
    points = places.shape[-1]
    spread = support.shape[1]
    group = math.gcd(rows, 16)

    def one_group(inputs):
        where, which = inputs
        return kernel_block(where[:, None], struct_points[which])

    kernels = lax.map(
        one_group, (places.reshape(-1, group, 3, points), support.reshape(-1, group, spread))
    )
    return kernels.reshape(rows, spread, points, points)


def owner_motion(kernels, support, field_values):
    return jnp.einsum("gkij,gkcj->gci", kernels, field_values[support], precision=TOP_PRECISION)


def owner_loads(kernels, support, blocks, traction):
    flux_terms = jnp.einsum("gkij,gci->gkcj", kernels, traction, precision=TOP_PRECISION)
    selector = (support[:, :, None] == jnp.arange(blocks, dtype=jnp.int32)[None, None, :]).astype(
        jnp.float32
    )
    return jnp.einsum("rke,rkcj->ecj", selector, flux_terms, precision=TOP_PRECISION)


def route_coords(geometry, support):
    moved_geometry, moved_support = (
        lax.all_to_all(geometry, ("fx", "fy"), split_axis=0, concat_axis=0, tiled=True),
        lax.all_to_all(support, ("fx", "fy"), split_axis=0, concat_axis=0, tiled=True),
    )
    return (moved_geometry, moved_support)


def route_field(values):
    return lax.all_to_all(values, ("fx", "fy"), split_axis=0, concat_axis=0, tiled=True)


def global_sums(values):
    return lax.psum(values, ("fx", "fy"))


def stiffness(field_values, couplings, sparsity_layout, selector, diagonal):
    blocks = field_values.shape[0]
    scale = 1.0 / (2.0 * couplings.shape[1] * couplings.shape[2])
    flux_terms = jnp.einsum("aosq,avs->aovq", couplings, field_values, precision=TOP_PRECISION)
    shipped = jnp.einsum("bke,bkdj->edj", selector, flux_terms, precision=TOP_PRECISION)
    stacked = jnp.concatenate([shipped, field_values], axis=0)
    extended = with_halo(stacked, ((("fx", "fy"), 0),), blocks)
    prior_iterate = extended[:blocks]
    later = extended[-blocks:]
    forward_pass = jnp.einsum(
        "hzwm,hzlm->hlw", couplings, prior_iterate[sparsity_layout], precision=TOP_PRECISION
    )
    return diagonal[:, None, :] * field_values - scale * (forward_pass + later)


def conjugate(start, rhs, operate):
    residual = rhs - operate(start)
    solution = start
    direction = residual
    norm_now = global_sums(jnp.stack([jnp.sum(residual * residual)]))[0]
    for count in range(CG_ITERS):
        image = operate(direction)
        alpha = norm_now / global_sums(jnp.stack([jnp.sum(direction * image)]))[0]
        solution = solution + alpha * direction
        residual = residual - alpha * image
        if count + 1 < CG_ITERS:
            norm_next = global_sums(jnp.stack([jnp.sum(residual * residual)]))[0]
            direction = residual + norm_next / norm_now * direction
            norm_now = norm_next
    return solution


def newton_update(response, gram, projected, responses):
    lower = jnp.linalg.cholesky(gram)
    middle = lax.linalg.triangular_solve(lower, projected[:, None], left_side=True, lower=True)
    weights = lax.linalg.triangular_solve(
        lower, middle, left_side=True, lower=True, transpose_a=True
    )[:, 0]
    return response - jnp.einsum("h,hbdp->bdp", weights, responses, precision=TOP_PRECISION)


def on_device(
    fluid_state,
    surface_points,
    surface_normals,
    owner_ids,
    support_ids,
    struct_points,
    couplings,
    coupling_pattern,
    stiff_diagonal,
    struct_load,
    predicted,
    hist_residual,
    hist_response,
):
    rows_fx = lax.axis_size("fx")
    rows_fy = lax.axis_size("fy")
    devices = rows_fx * rows_fy
    surface_count = owner_ids.shape[0]
    capacity = max(2, 2 * surface_count // devices)
    owners = owner_ids[:, 0]
    chosen = (owners[:, None] == jnp.arange(devices, dtype=jnp.int32)[None, :]).astype(jnp.int32)
    slots = owners * capacity + jnp.sum((jnp.cumsum(chosen, axis=0) - chosen) * chosen, axis=1)
    width = devices * capacity

    def pack(values):
        return jnp.zeros((width,) + values.shape[1:], values.dtype).at[slots].set(values)

    owner_geometry, owner_support = route_coords(pack(surface_points), pack(support_ids))
    kernels = owner_kernels(owner_geometry, owner_support, struct_points)
    blocks = couplings.shape[0]
    selector = (
        coupling_pattern[:, :, None] == jnp.arange(blocks, dtype=jnp.int32)[None, None, :]
    ).astype(jnp.float32)

    def operate(field_values):
        return stiffness(field_values, couplings, coupling_pattern, selector, stiff_diagonal)

    horizontal = horizontal_terms(fluid_state)
    estimate = predicted
    differences = hist_residual
    responses = hist_response
    last_residual = predicted
    last_response = predicted
    new_state = fluid_state
    residual = predicted
    for count in range(COUPLE):
        motion_slots = owner_motion(kernels, owner_support, estimate)
        motion = route_field(motion_slots)[slots]
        wall = WALL_SPEED * jnp.tanh(WALL_GAIN * jnp.sum(surface_normals * motion, axis=1))
        new_state = fluid_state - STEP_RATIO * (horizontal + vertical_terms(fluid_state, wall))
        pressure = state_pressure(new_state[:, 0])
        traction = -LOAD_SCALE * (pressure - PRESSURE_REF)[:, None, :] * surface_normals
        owner_traction = route_field(pack(traction))
        loads = owner_loads(kernels, owner_support, blocks, owner_traction)
        response = conjugate(estimate, struct_load + loads, operate)
        residual = response - estimate
        if count > 0:
            differences = jnp.concatenate(
                [differences[1:], (residual - last_residual)[None]], axis=0
            )
            responses = jnp.concatenate([responses[1:], (response - last_response)[None]], axis=0)
        last_residual = residual
        last_response = response
        gram = jnp.einsum("hbdp,gbdp->hg", differences, differences, precision=TOP_PRECISION)
        projected = jnp.einsum("hbdp,bdp->h", differences, residual, precision=TOP_PRECISION)
        totals = global_sums(jnp.concatenate([gram, projected[:, None]], axis=1))
        estimate = newton_update(response, totals[:, :-1], totals[:, -1], responses)
    return (new_state, estimate, residual)


def solution(mesh):
    placed = (
        P(None, None, "fx", "fy"),
        P(("fx", "fy"), None, None),
        P(("fx", "fy"), None, None),
        P(("fx", "fy"), None),
        P(("fx", "fy"), None),
        P(("fx", "fy"), None, None),
        P(("fx", "fy"), None, None, None),
        P(("fx", "fy"), None),
        P(("fx", "fy"), None),
        P(("fx", "fy"), None, None),
        P(("fx", "fy"), None, None),
        P(None, ("fx", "fy"), None, None),
        P(None, ("fx", "fy"), None, None),
    )
    return jax.shard_map(
        on_device,
        mesh=mesh,
        in_specs=placed,
        out_specs=(
            P(None, None, "fx", "fy"),
            P(("fx", "fy"), None, None),
            P(("fx", "fy"), None, None),
        ),
        check_vma=False,
    )
```

profile of v0, /device:TPU:1, one launch (start us, length us, event | category | flops | bytes accessed | tf_op | source)
XLA Modules:
  0.0 1005.2 jit_solution(8151141601063758827)
XLA Ops:
  6.5 11.5 %all-to-all-start = ((s32[128,2,2]{1,2,0:T(2,128)}), s32[128,2,2]{1,2,0:T(2,128)S(1)}, u32[]{:S(2)}, u32[]{:S(2)}) async-start(s32[128,2,2]{1,2,0:T(2,128)} %copy.261), calls=%async_computation | async-start | bytes 262144 | tf_op jit(solution)/shard_map/all_to_all | solution.py:134
  32.7 12.5 %scatter_fusion = f32[256,3,128]{2,1,0:T(4,128)} fusion(f32[256,3,128]{2,1,0:T(4,128)} %broadcast.438.clone, s32[128]{0:T(128)S(1)} %fusion.166, f32[128,3,128]{2,1,0:T(4,128)S(1)} %copy.265), kind=kCustom, calls=%fused_computation.12 | custom fusion | bytes 590336 | tf_op jit(solution)/shard_map/scatter | solution.py:214
  45.2 15.0 %all-to-all-start.1 = ((f32[256,3,128]{2,1,0:T(4,128)}), f32[256,3,128]{2,1,0:T(4,128)}, u32[]{:S(2)}, u32[]{:S(2)}) async-start(f32[256,3,128]{2,1,0:T(4,128)} %scatter_fusion), calls=%async_computation.1 | async-start | bytes 1048576 | tf_op jit(solution)/shard_map/all_to_all | solution.py:133
  112.6 69.3 %while.20 = (s32[]{:T(128)}, f32[16,16,2,128,128]{4,3,2,1,0:T(8,128)}, f32[16,16,3,128]{3,1,2,0:T(8,128)}, s32[16,16,2]{1,0,2:T(8,128)S(1)}, f32[8,3,128]{2,1,0:T(4,128)S(1)}, /*index=5*/s32[]{:T(128)}) while((s32[]{:T(128)}, f32[16,16,2,128,128]{4,3,2,1,0:T(8,128)}, f32[16,16,3,128]{3,1,2,0:T(8,128)}, s32[16,16,2]{1,0,2:T(8,128)S(1)}, ...), condition=%wide.region_5.6_spmd, body=%wide.region_4.5_spmd.sunk | while | flops 8389730 | bytes 2471257 | solution.py:113
  182.0 32.0 %convolution_bitcast_fusion.3 = f32[256,3,128]{2,1,0:T(4,128)} fusion(f32[256,2,128,128]{3,2,1,0:T(8,128)} %bitcast.465, f32[256,2,3,128]{3,1,0,2:T(2,128)S(1)} %bitcast.471), kind=kOutput, calls=%fused_computation.76 | convolution fusion | flops 301989888 | bytes 34734080 | tf_op jit(solution)/shard_map/gkij,gkcj->gci/dot_general | solution.py:120
  213.9 10.2 %all-to-all-start.2 = ((f32[256,3,128]{2,1,0:T(4,128)}), f32[256,3,128]{2,1,0:T(4,128)}, u32[]{:S(2)}, u32[]{:S(2)}) async-start(f32[256,3,128]{2,1,0:T(4,128)} %convolution_bitcast_fusion.3), calls=%async_computation.2 | async-start | bytes 1048576 | tf_op jit(solution)/shard_map/all_to_all | solution.py:140
  224.2 11.7 %fusion.4 = f32[5,8,128,129]{3,2,1,0:T(8,128)} fusion(f32[5,8,130,1]{3,2,1,0:T(8,128)} %copy.255, f32[5,8,1,128]{3,2,1,0:T(1,128)S(1)} %bitcast.482, f32[5,8,128,128]{3,2,1,0:T(8,128)} %param.40, f32[5,8,1,128]{3,2,1,0:T(1,128)S(1)} %bitcast.487, f32[5,8,130,1]{3,2,1,0:T(8,128)} %copy.256, f32[5,8,128,130]{3,2,1,0:T(8,128)} %fusion.25, f32[8,128,129]{2,1,0:T(8,128)} %fusion.24), kind=kLoop, calls=%fused_computation.29 | loop fusion | flops 7265280 | bytes 11158144 | tf_op jit(solution)/shard_map/sub | solution.py:53
  252.1 12.4 %scatter_fusion.1 = f32[256,3,128]{2,1,0:T(4,128)} fusion(f32[256,3,128]{2,1,0:T(4,128)} %broadcast.438.clone.1, s32[128]{0:T(128)S(1)} %fusion.166, f32[128,3,128]{2,1,0:T(4,128)S(1)} %copy.273), kind=kCustom, calls=%fused_computation.13 | custom fusion | bytes 590336 | tf_op jit(solution)/shard_map/scatter | solution.py:214
  264.5 9.2 all-to-all-start.3
  276.7 10.5 %all-to-all-done.3 = f32[256,3,128]{2,1,0:T(4,128)S(1)} async-done(((f32[256,3,128]{2,1,0:T(4,128)}), f32[256,3,128]{2,1,0:T(4,128)S(1)}, u32[]{:S(2)}, u32[]{:S(2)}) %all-to-all-start.3) | async-done | bytes 393248 | tf_op jit(solution)/shard_map/all_to_all | solution.py:140
  287.2 19.6 %convolution_bitcast_fusion.1 = f32[256,2,3,128]{3,2,1,0:T(4,128)S(1)} fusion(f32[256,2,128,128]{3,2,1,0:T(8,128)} %bitcast.466, f32[256,3,128]{2,1,0:T(4,128)S(1)} %all-to-all-done.3), kind=kOutput, calls=%fused_computation.74 | convolution fusion | flops 301989888 | bytes 34734080 | tf_op jit(solution)/shard_map/gkij,gci->gkcj/dot_general | solution.py:124
  314.2 71.7 %all-reduce.1 = (f32[1]{0:T(128)}, f32[1]{0:T(128)}) all-reduce(f32[1]{0:T(128)} %bitcast.55, f32[1]{0:T(128)} %bitcast.63), channel_id=1, replica_groups=mesh['fx'=16,'fy'=8] {'fx','fy'}, use_global_device_ids=true, to_apply=%region_9.10 | all-reduce | flops 2 | bytes 16 | tf_op jit(solution)/shard_map/psum | solution.py:144
  388.0 62.7 %psum.72 = f32[1]{0:T(128)} all-reduce(f32[1]{0:T(128)} %bitcast.65), channel_id=1, replica_groups=mesh['fx'=16,'fy'=8] {'fx','fy'}, use_global_device_ids=true, to_apply=%region_13.14 | all-reduce | flops 1 | bytes 8 | tf_op jit(solution)/shard_map/psum | solution.py:144
  459.2 70.4 %psum.73 = f32[1]{0:T(128)} all-reduce(f32[1]{0:T(128)} %bitcast.74), channel_id=1, replica_groups=mesh['fx'=16,'fy'=8] {'fx','fy'}, use_global_device_ids=true, to_apply=%region_15.16 | all-reduce | flops 1 | bytes 8 | tf_op jit(solution)/shard_map/psum | solution.py:144
  531.3 62.6 %psum.74 = f32[8,9]{0,1:T(8,128)S(1)} all-reduce(f32[8,9]{0,1:T(8,128)S(1)} %pad_maximum_fusion.17), channel_id=1, replica_groups=mesh['fx'=16,'fy'=8] {'fx','fy'}, use_global_device_ids=true, to_apply=%region_16.17 | all-reduce | flops 72 | bytes 576 | tf_op jit(solution)/shard_map/psum | solution.py:144
  599.2 31.6 %convolution_bitcast_fusion.2 = f32[256,3,128]{2,1,0:T(4,128)} fusion(f32[256,2,3,128]{3,2,1,0:T(4,128)S(1)} %bitcast.472, f32[256,2,128,128]{3,2,1,0:T(8,128)} %bitcast.467), kind=kOutput, calls=%fused_computation.75 | convolution fusion | flops 301989888 | bytes 34734080 | tf_op jit(solution)/shard_map/gkij,gkcj->gci/dot_general | solution.py:120
  639.1 10.9 %all-to-all-done.4 = f32[256,3,128]{2,1,0:T(4,128)S(1)} async-done(((f32[256,3,128]{2,1,0:T(4,128)}), f32[256,3,128]{2,1,0:T(4,128)S(1)}, u32[]{:S(2)}, u32[]{:S(2)}) %all-to-all-start.4) | async-done | bytes 393248 | tf_op jit(solution)/shard_map/all_to_all | solution.py:140
  664.4 12.4 %scatter_fusion.2 = f32[256,3,128]{2,1,0:T(4,128)} fusion(f32[256,3,128]{2,1,0:T(4,128)} %broadcast.438, s32[128]{0:T(128)S(1)} %copy-done.27, f32[128,3,128]{2,1,0:T(4,128)S(1)} %copy.296), kind=kCustom, calls=%fused_computation.14 | custom fusion | bytes 590336 | tf_op jit(solution)/shard_map/scatter | solution.py:214
  686.7 8.3 all-to-all-done.5
  695.0 19.6 %convolution_bitcast_fusion = f32[256,2,3,128]{3,2,1,0:T(4,128)S(1)} fusion(f32[256,2,128,128]{3,2,1,0:T(8,128)} %bitcast.468, f32[256,3,128]{2,1,0:T(4,128)S(1)} %all-to-all-done.5), kind=kOutput, calls=%fused_computation.73 | convolution fusion | flops 301989888 | bytes 34734080 | tf_op jit(solution)/shard_map/gkij,gci->gkcj/dot_general | solution.py:124
  721.3 71.7 %all-reduce = (f32[1]{0:T(128)}, f32[1]{0:T(128)}) all-reduce(f32[1]{0:T(128)} %bitcast.119, f32[1]{0:T(128)} %bitcast.127), channel_id=1, replica_groups=mesh['fx'=16,'fy'=8] {'fx','fy'}, use_global_device_ids=true, to_apply=%region_22.26 | all-reduce | flops 2 | bytes 16 | tf_op jit(solution)/shard_map/psum | solution.py:144
  795.0 62.5 %psum.77 = f32[1]{0:T(128)} all-reduce(f32[1]{0:T(128)} %bitcast.129), channel_id=1, replica_groups=mesh['fx'=16,'fy'=8] {'fx','fy'}, use_global_device_ids=true, to_apply=%region_26.30 | all-reduce | flops 1 | bytes 8 | tf_op jit(solution)/shard_map/psum | solution.py:144
  866.1 70.4 %psum.78 = f32[1]{0:T(128)} all-reduce(f32[1]{0:T(128)} %bitcast.138), channel_id=1, replica_groups=mesh['fx'=16,'fy'=8] {'fx','fy'}, use_global_device_ids=true, to_apply=%region_28.32 | all-reduce | flops 1 | bytes 8 | tf_op jit(solution)/shard_map/psum | solution.py:144
  938.5 62.6 %psum.79 = f32[8,9]{0,1:T(8,128)S(1)} all-reduce(f32[8,9]{0,1:T(8,128)S(1)} %pad_maximum_fusion.18), channel_id=1, replica_groups=mesh['fx'=16,'fy'=8] {'fx','fy'}, use_global_device_ids=true, to_apply=%region_29.33 | all-reduce | flops 72 | bytes 576 | tf_op jit(solution)/shard_map/psum | solution.py:144
  (422 shorter events, 232.6 us)
Async XLA Ops:
  6.5 38.7 %all-to-all-start = ((s32[128,2,2]{1,2,0:T(2,128)}), s32[128,2,2]{1,2,0:T(2,128)S(1)}, u32[]{:S(2)}, u32[]{:S(2)}) async-start(s32[128,2,2]{1,2,0:T(2,128)} %copy.261), calls=%async_computation | async-start | bytes 262144 | tf_op jit(solution)/shard_map/all_to_all | solution.py:134
  19.6 43.4 %collective-permute-start.1 = (f32[5,8,1,128]{3,1,2,0:T(8,128)}, f32[5,8,1,128]{3,1,2,0:T(8,128)S(1)}, u32[]{:S(2)}, u32[]{:S(2)}) collective-permute-start(f32[5,8,1,128]{3,1,2,0:T(8,128)} %bitcast.176), channel_id=1, source_target_pairs={{8,0},{16,8},{24,16},{32,24},{40,32},{48,40},{56,48},{64,56},{72,6... | collective-permute-start | bytes 61448 | tf_op jit(solution)/shard_map/ppermute | solution.py:27
  25.0 38.0 %collective-permute-start = (f32[5,8,1,128]{3,1,2,0:T(8,128)}, f32[5,8,1,128]{3,1,2,0:T(8,128)S(1)}, u32[]{:S(2)}, u32[]{:S(2)}) collective-permute-start(f32[5,8,1,128]{3,1,2,0:T(8,128)} %bitcast.175), channel_id=1, source_target_pairs={{0,8},{8,16},{16,24},{24,32},{32,40},{40,48},{48,56},{56,64},{64,7... | collective-permute-start | bytes 61448 | tf_op jit(solution)/shard_map/ppermute | solution.py:25
  27.7 279.1 %collective-permute-start.5 = (f32[8,3,128]{2,0,1:T(8,128)}, f32[8,3,128]{2,0,1:T(8,128)}, u32[]{:S(2)}, u32[]{:S(2)}) collective-permute-start(f32[8,3,128]{2,0,1:T(8,128)} %convolution_bitcast_fusion.22), channel_id=1, source_target_pairs={{1,0},{2,1},{3,2},{4,3},{5,4},{6,5},{7,6},{8,7},{9,8},{10,9},{11,1... | collective-permute-start | bytes 36872 | tf_op jit(solution)/shard_map/ppermute | solution.py:27
  28.3 245.9 %collective-permute-start.4 = (f32[8,3,128]{2,1,0:T(4,128)S(1)}, f32[8,3,128]{2,1,0:T(4,128)S(1)}, u32[]{:S(2)}, u32[]{:S(2)}) collective-permute-start(f32[8,3,128]{2,1,0:T(4,128)S(1)} %copy.275), channel_id=1, source_target_pairs={{0,1},{1,2},{2,3},{3,4},{4,5},{5,6},{6,7},{7,8},{8,9},{9,10},{10,1... | collective-permute-start | bytes 36872 | tf_op jit(solution)/shard_map/ppermute | solution.py:25
  45.2 65.6 %all-to-all-start.1 = ((f32[256,3,128]{2,1,0:T(4,128)}), f32[256,3,128]{2,1,0:T(4,128)}, u32[]{:S(2)}, u32[]{:S(2)}) async-start(f32[256,3,128]{2,1,0:T(4,128)} %scatter_fusion), calls=%async_computation.1 | async-start | bytes 1048576 | tf_op jit(solution)/shard_map/all_to_all | solution.py:133
  73.7 13.5 %collective-permute-start.2 = (f32[5,8,130,1]{2,1,3,0:T(8,128)S(1)}, f32[5,8,130,1]{2,1,3,0:T(8,128)}, u32[]{:S(2)}, u32[]{:S(2)}) collective-permute-start(f32[5,8,130,1]{2,1,3,0:T(8,128)S(1)} %copy.253), channel_id=1, source_target_pairs={{0,1},{1,2},{2,3},{3,4},{4,5},{5,6},{6,7},{7,0},{8,9},{9,10},{10,1... | collective-permute-start | bytes 62408 | tf_op jit(solution)/shard_map/ppermute | solution.py:25
  79.2 11.2 %collective-permute-start.3 = (f32[5,8,130,1]{2,1,3,0:T(8,128)}, f32[5,8,130,1]{2,1,3,0:T(8,128)}, u32[]{:S(2)}, u32[]{:S(2)}) collective-permute-start(f32[5,8,130,1]{2,1,3,0:T(8,128)} %copy.254), channel_id=1, source_target_pairs={{1,0},{2,1},{3,2},{4,3},{5,4},{6,5},{7,6},{0,7},{9,8},{10,9},{11,1... | collective-permute-start | bytes 62408 | tf_op jit(solution)/shard_map/ppermute | solution.py:27
  213.9 23.2 %all-to-all-start.2 = ((f32[256,3,128]{2,1,0:T(4,128)}), f32[256,3,128]{2,1,0:T(4,128)}, u32[]{:S(2)}, u32[]{:S(2)}) async-start(f32[256,3,128]{2,1,0:T(4,128)} %convolution_bitcast_fusion.3), calls=%async_computation.2 | async-start | bytes 1048576 | tf_op jit(solution)/shard_map/all_to_all | solution.py:140
  264.5 22.7 %all-to-all-start.3 = ((f32[256,3,128]{2,1,0:T(4,128)}), f32[256,3,128]{2,1,0:T(4,128)S(1)}, u32[]{:S(2)}, u32[]{:S(2)}) async-start(f32[256,3,128]{2,1,0:T(4,128)} %scatter_fusion.1), calls=%async_computation.3 | async-start | bytes 1048576 | tf_op jit(solution)/shard_map/all_to_all | solution.py:140
  308.0 2.5 collective-permute-start.6
  310.5 3.1 collective-permute-start.7
  312.9 283.9 %copy-start.17 = (f32[8,8,3,128]{3,1,2,0:T(8,128)S(1)}, f32[8,8,3,128]{3,1,2,0:T(8,128)}, u32[]{:S(2)}) copy-start(f32[8,8,3,128]{3,1,2,0:T(8,128)} %param.52) | copy-start | bytes 294916
  452.1 3.0 collective-permute-start.8
  455.1 3.4 collective-permute-start.9
  630.9 19.1 %all-to-all-start.4 = ((f32[256,3,128]{2,1,0:T(4,128)}), f32[256,3,128]{2,1,0:T(4,128)S(1)}, u32[]{:S(2)}, u32[]{:S(2)}) async-start(f32[256,3,128]{2,1,0:T(4,128)} %convolution_bitcast_fusion.2), calls=%async_computation.4 | async-start | bytes 1048576 | tf_op jit(solution)/shard_map/all_to_all | solution.py:140
  637.1 47.1 %collective-permute-start.10 = (f32[8,3,128]{2,0,1:T(8,128)S(1)}, f32[8,3,128]{2,0,1:T(8,128)S(1)}, u32[]{:S(2)}, u32[]{:S(2)}) collective-permute-start(f32[8,3,128]{2,0,1:T(8,128)S(1)} %bitcast_subtract_fusion.1), channel_id=1, source_target_pairs={{0,1},{1,2},{2,3},{3,4},{4,5},{5,6},{6,7},{7,8},{8,9},{9,10},{10,1... | collective-permute-start | bytes 36872 | tf_op jit(solution)/shard_map/ppermute | solution.py:25
  676.8 18.1 %all-to-all-start.5 = ((f32[256,3,128]{2,1,0:T(4,128)}), f32[256,3,128]{2,1,0:T(4,128)S(1)}, u32[]{:S(2)}, u32[]{:S(2)}) async-start(f32[256,3,128]{2,1,0:T(4,128)} %scatter_fusion.2), calls=%async_computation.5 | async-start | bytes 1048576 | tf_op jit(solution)/shard_map/all_to_all | solution.py:140
  682.8 31.9 %collective-permute-start.11 = (f32[8,3,128]{2,0,1:T(8,128)S(1)}, f32[8,3,128]{2,0,1:T(8,128)S(1)}, u32[]{:S(2)}, u32[]{:S(2)}) collective-permute-start(f32[8,3,128]{2,0,1:T(8,128)S(1)} %convolution_bitcast_fusion.18), channel_id=1, source_target_pairs={{1,0},{2,1},{3,2},{4,3},{5,4},{6,5},{7,6},{8,7},{9,8},{10,9},{11,1... | collective-permute-start | bytes 36872 | tf_op jit(solution)/shard_map/ppermute | solution.py:27
  715.1 2.5 collective-permute-start.12
  717.5 3.1 collective-permute-start.13
  720.0 284.1 %slice-start.2 = ((f32[8,8,3,128]{3,1,2,0:T(8,128)}), f32[7,8,3,128]{3,1,2,0:T(8,128)S(1)}, s32[]{:S(2)}) async-start(f32[8,8,3,128]{3,1,2,0:T(8,128)} %param.52), calls=%async_computation.8 | async-start | bytes 172032 | tf_op jit(solution)/shard_map/slice | solution.py:249
  858.9 3.2 collective-permute-start.14
  862.0 3.4 collective-permute-start.15
  (30 other events, 897.5 us)
where the time goes:
time: 1010 us
  blocking collectives  535 us (53%)
  matrix products  127 us (13%)
  local copies, waits for them, and re-layouts  113 us (11%)
  other arithmetic  113 us (11%)
  starting transfers between devices  74.2 us (7%)
  waiting for transfers between devices  34.2 us (3%)
    psum x8, blocking collectives, global_sums(): return lax.psum(values, ('fx', 'fy'))  535 us
    dot_general x2, matrix products, owner_motion(): jnp.einsum('gkij,gkcj->gci', kernels, field_values[support], precision=TO...  63.6 us
    dynamic_update_slice x16, other arithmetic, owner_kernels(): lax.map(one_group, (places.reshape(-1, group, 3, points), support.reshape...  43.5 us
    dot_general x2, matrix products, owner_loads(): jnp.einsum('gkij,gci->gkcj', kernels, traction, precision=TOP_PRECISION)  39.3 us
    scatter x4, local copies, waits for them, and re-layouts, pack(): jnp.zeros((width,) + values.shape[1:], values.dtype).at[slots].set(values)  38.3 us
    all_to_all x4, waiting for transfers between devices, route_field(): lax.all_to_all(values, ('fx', 'fy'), split_axis=0, concat_axis=0, tiled=T...  30.9 us
    all_to_all x4, starting transfers between devices, route_field(): lax.all_to_all(values, ('fx', 'fy'), split_axis=0, concat_axis=0, tiled=T...  29.5 us
  transfers between devices with their start and end apart: 22, of which 8 were waited for; matrix products, arithmetic and copies ran while one was open for 29% of the time, Pallas kernels for 0%

commit v1 on v0

--- a/solution.py
+++ b/solution.py
@@ -3,6 +3,7 @@
 import jax.numpy as jnp
 from jax import lax
 from jax.sharding import PartitionSpec as P
+from jax.lax import psum
 
 CG_ITERS = 2
 COUPLE = 2
@@ -13,6 +14,9 @@
 LOAD_SCALE = 4.0
 PRESSURE_REF = 0.98
 RADIUS = 1.0
+part_ratios = lambda group_axis, axis_key, matrix: psum(
+    psum(matrix, axis_name=group_axis), axis_key
+)
 
 
 def with_halo(cells, sides, width):
@@ -141,7 +145,7 @@
 
 
 def global_sums(values):
-    return lax.psum(values, ("fx", "fy"))
+    return part_ratios("fx", "fy", values)
 
 
 def stiffness(field_values, couplings, sparsity_layout, selector, diagonal):

time: 1010 us -> 899 us (0.89)
  blocking collectives: 535 us -> 425 us
    psum x8 -> x16, blocking collectives: 535 us -> 425 us  [the longest x8 243 us: psum(matrix, axis_name=group_axis)]
  transfers between devices with their start and end apart: 22 -> 22, of which waited for: 8 -> 6; matrix products, arithmetic and copies ran while one was open for 29% -> 32% of each run, Pallas kernels for 0% -> 0%
where the time goes in v1:
time: 899 us; the launch traced here: 891 us
  blocking collectives  425 us (47%)
  matrix products  127 us (14%)
  other arithmetic  113 us (13%)
  local copies, waits for them, and re-layouts  112 us (12%)
  starting transfers between devices  70.8 us (8%)
  waiting for transfers between devices  33.6 us (4%)
  between operations  9.95 us (1%)
    psum x8, blocking collectives, psum(matrix, axis_name=group_axis)  243 us
    psum x8, blocking collectives, psum(psum(matrix, axis_name=group_axis), axis_key)  182 us
    dot_general x2, matrix products, owner_motion(): jnp.einsum('gkij,gkcj->gci', kernels, field_values[support], precision=TO...  63.6 us
    dynamic_update_slice x16, other arithmetic, owner_kernels(): lax.map(one_group, (places.reshape(-1, group, 3, points), support.reshape...  43.5 us
    dot_general x2, matrix products, owner_loads(): jnp.einsum('gkij,gci->gkcj', kernels, traction, precision=TOP_PRECISION)  39.3 us
    scatter x4, local copies, waits for them, and re-layouts, pack(): jnp.zeros((width,) + values.shape[1:], values.dtype).at[slots].set(values)  38.3 us
    all_to_all x4, waiting for transfers between devices, route_field(): lax.all_to_all(values, ('fx', 'fy'), split_axis=0, concat_axis=0, tiled=T...  32.2 us
    all_to_all x4, starting transfers between devices, route_field(): lax.all_to_all(values, ('fx', 'fy'), split_axis=0, concat_axis=0, tiled=T...  28 us
  transfers between devices with their start and end apart: 22, of which 6 were waited for; matrix products, arithmetic and copies ran while one was open for 32% of the time, Pallas kernels for 0%

profile of v1, /device:TPU:1, one launch (start us, length us, event | category | flops | bytes accessed | tf_op | source)
XLA Modules:
  0.0 890.9 jit_solution(4745343657798626561)
XLA Ops:
  32.5 12.5 %scatter_fusion = f32[256,3,128]{2,1,0:T(4,128)} fusion(f32[256,3,128]{2,1,0:T(4,128)} %broadcast.438.clone, s32[128]{0:T(128)S(1)} %fusion.166, f32[128,3,128]{2,1,0:T(4,128)S(1)} %copy.265), kind=kCustom, calls=%fused_computation.12 | custom fusion | bytes 590336 | tf_op jit(solution)/shard_map/scatter | solution.py:218
  45.0 14.9 %all-to-all-start.1 = ((f32[256,3,128]{2,1,0:T(4,128)}), f32[256,3,128]{2,1,0:T(4,128)}, u32[]{:S(2)}, u32[]{:S(2)}) async-start(f32[256,3,128]{2,1,0:T(4,128)} %scatter_fusion), calls=%async_computation.1 | async-start | bytes 1048576 | tf_op jit(solution)/shard_map/all_to_all | solution.py:137
  112.3 69.4 %while.20 = (s32[]{:T(128)}, f32[16,16,2,128,128]{4,3,2,1,0:T(8,128)}, f32[16,16,3,128]{3,1,2,0:T(8,128)}, s32[16,16,2]{1,0,2:T(8,128)S(1)}, f32[8,3,128]{2,1,0:T(4,128)S(1)}, /*index=5*/s32[]{:T(128)}) while((s32[]{:T(128)}, f32[16,16,2,128,128]{4,3,2,1,0:T(8,128)}, f32[16,16,3,128]{3,1,2,0:T(8,128)}, s32[16,16,2]{1,0,2:T(8,128)S(1)}, ...), condition=%wide.region_5.6_spmd, body=%wide.region_4.5_spmd.sunk | while | flops 8389730 | bytes 2471257 | solution.py:117
  181.7 32.0 %convolution_bitcast_fusion.3 = f32[256,3,128]{2,1,0:T(4,128)} fusion(f32[256,2,128,128]{3,2,1,0:T(8,128)} %bitcast.465, f32[256,2,3,128]{3,1,0,2:T(2,128)S(1)} %bitcast.471), kind=kOutput, calls=%fused_computation.76 | convolution fusion | flops 301989888 | bytes 34734080 | tf_op jit(solution)/shard_map/gkij,gkcj->gci/dot_general | solution.py:124
  251.8 12.5 %scatter_fusion.1 = f32[256,3,128]{2,1,0:T(4,128)} fusion(f32[256,3,128]{2,1,0:T(4,128)} %broadcast.438.clone.1, s32[128]{0:T(128)S(1)} %fusion.166, f32[128,3,128]{2,1,0:T(4,128)S(1)} %copy.273), kind=kCustom, calls=%fused_computation.13 | custom fusion | bytes 590336 | tf_op jit(solution)/shard_map/scatter | solution.py:218
  286.9 19.6 %convolution_bitcast_fusion.1 = f32[256,2,3,128]{3,2,1,0:T(4,128)S(1)} fusion(f32[256,2,128,128]{3,2,1,0:T(8,128)} %bitcast.466, f32[256,3,128]{2,1,0:T(4,128)S(1)} %all-to-all-done.3), kind=kOutput, calls=%fused_computation.74 | convolution fusion | flops 301989888 | bytes 34734080 | tf_op jit(solution)/shard_map/gkij,gci->gkcj/dot_general | solution.py:128
  313.9 30.5 %all-reduce.1 = (f32[1]{0:T(128)}, f32[1]{0:T(128)}) all-reduce(f32[1]{0:T(128)} %bitcast.55, f32[1]{0:T(128)} %bitcast.63), channel_id=1, replica_groups=mesh['fx'=16,'fy'=8] {'fx'}, use_global_device_ids=true, to_apply=%region_9.10 | all-reduce | flops 2 | bytes 16 | tf_op jit(solution)/shard_map/psum | solution.py:18
  344.4 24.7 %all-reduce.3 = (f32[1]{0:T(128)}, f32[1]{0:T(128)}) all-reduce(f32[1]{0:T(128)} %get-tuple-element.196, f32[1]{0:T(128)} %get-tuple-element.197), channel_id=1, replica_groups=mesh['fx'=16,'fy'=8] {'fy'}, use_global_device_ids=true, to_apply=%region_10.11 | all-reduce | flops 2 | bytes 16 | tf_op jit(solution)/shard_map/psum | solution.py:17
  371.0 30.9 %psum.144 = f32[1]{0:T(128)} all-reduce(f32[1]{0:T(128)} %bitcast.65), channel_id=1, replica_groups=mesh['fx'=16,'fy'=8] {'fx'}, use_global_device_ids=true, to_apply=%region_15.16 | all-reduce | flops 1 | bytes 8 | tf_op jit(solution)/shard_map/psum | solution.py:18
  401.9 20.3 %psum.145 = f32[1]{0:T(128)} all-reduce(f32[1]{0:T(128)} %psum.144), channel_id=1, replica_groups=mesh['fx'=16,'fy'=8] {'fy'}, use_global_device_ids=true, to_apply=%region_16.17 | all-reduce | flops 1 | bytes 8 | tf_op jit(solution)/shard_map/psum | solution.py:17
  428.8 29.3 %psum.146 = f32[1]{0:T(128)} all-reduce(f32[1]{0:T(128)} %bitcast.74), channel_id=1, replica_groups=mesh['fx'=16,'fy'=8] {'fx'}, use_global_device_ids=true, to_apply=%region_18.19 | all-reduce | flops 1 | bytes 8 | tf_op jit(solution)/shard_map/psum | solution.py:18
  458.4 26.5 %psum.147 = f32[1]{0:T(128)} all-reduce(f32[1]{0:T(128)} %psum.146), channel_id=1, replica_groups=mesh['fx'=16,'fy'=8] {'fy'}, use_global_device_ids=true, to_apply=%region_19.20 | all-reduce | flops 1 | bytes 8 | tf_op jit(solution)/shard_map/psum | solution.py:17
  486.6 31.0 %psum.148 = f32[8,9]{0,1:T(8,128)S(1)} all-reduce(f32[8,9]{0,1:T(8,128)S(1)} %pad_maximum_fusion.17), channel_id=1, replica_groups=mesh['fx'=16,'fy'=8] {'fx'}, use_global_device_ids=true, to_apply=%region_20.21 | all-reduce | flops 72 | bytes 576 | tf_op jit(solution)/shard_map/psum | solution.py:18
  517.7 19.6 %psum.149 = f32[8,9]{0,1:T(8,128)S(1)} all-reduce(f32[8,9]{0,1:T(8,128)S(1)} %psum.148), channel_id=1, replica_groups=mesh['fx'=16,'fy'=8] {'fy'}, use_global_device_ids=true, to_apply=%region_21.22 | all-reduce | flops 72 | bytes 576 | tf_op jit(solution)/shard_map/psum | solution.py:17
  542.6 31.6 %convolution_bitcast_fusion.2 = f32[256,3,128]{2,1,0:T(4,128)} fusion(f32[256,2,3,128]{3,2,1,0:T(4,128)S(1)} %bitcast.472, f32[256,2,128,128]{3,2,1,0:T(8,128)} %bitcast.467), kind=kOutput, calls=%fused_computation.75 | convolution fusion | flops 301989888 | bytes 34734080 | tf_op jit(solution)/shard_map/gkij,gkcj->gci/dot_general | solution.py:124
  637.1 19.6 %convolution_bitcast_fusion = f32[256,2,3,128]{3,2,1,0:T(4,128)S(1)} fusion(f32[256,2,128,128]{3,2,1,0:T(8,128)} %bitcast.468, f32[256,3,128]{2,1,0:T(4,128)S(1)} %all-to-all-done.5), kind=kOutput, calls=%fused_computation.73 | convolution fusion | flops 301989888 | bytes 34734080 | tf_op jit(solution)/shard_map/gkij,gci->gkcj/dot_general | solution.py:128
  663.4 30.4 %all-reduce = (f32[1]{0:T(128)}, f32[1]{0:T(128)}) all-reduce(f32[1]{0:T(128)} %bitcast.119, f32[1]{0:T(128)} %bitcast.127), channel_id=1, replica_groups=mesh['fx'=16,'fy'=8] {'fx'}, use_global_device_ids=true, to_apply=%region_27.31 | all-reduce | flops 2 | bytes 16 | tf_op jit(solution)/shard_map/psum | solution.py:18
  693.8 24.6 %all-reduce.2 = (f32[1]{0:T(128)}, f32[1]{0:T(128)}) all-reduce(f32[1]{0:T(128)} %get-tuple-element.194, f32[1]{0:T(128)} %get-tuple-element.195), channel_id=1, replica_groups=mesh['fx'=16,'fy'=8] {'fy'}, use_global_device_ids=true, to_apply=%region_28.32 | all-reduce | flops 2 | bytes 16 | tf_op jit(solution)/shard_map/psum | solution.py:17
  720.5 30.8 %psum.154 = f32[1]{0:T(128)} all-reduce(f32[1]{0:T(128)} %bitcast.129), channel_id=1, replica_groups=mesh['fx'=16,'fy'=8] {'fx'}, use_global_device_ids=true, to_apply=%region_33.37 | all-reduce | flops 1 | bytes 8 | tf_op jit(solution)/shard_map/psum | solution.py:18
  751.3 20.3 %psum.155 = f32[1]{0:T(128)} all-reduce(f32[1]{0:T(128)} %psum.154), channel_id=1, replica_groups=mesh['fx'=16,'fy'=8] {'fy'}, use_global_device_ids=true, to_apply=%region_34.38 | all-reduce | flops 1 | bytes 8 | tf_op jit(solution)/shard_map/psum | solution.py:17
  778.3 29.2 %psum.156 = f32[1]{0:T(128)} all-reduce(f32[1]{0:T(128)} %bitcast.138), channel_id=1, replica_groups=mesh['fx'=16,'fy'=8] {'fx'}, use_global_device_ids=true, to_apply=%region_36.40 | all-reduce | flops 1 | bytes 8 | tf_op jit(solution)/shard_map/psum | solution.py:18
  807.5 26.4 %psum.157 = f32[1]{0:T(128)} all-reduce(f32[1]{0:T(128)} %psum.156), channel_id=1, replica_groups=mesh['fx'=16,'fy'=8] {'fy'}, use_global_device_ids=true, to_apply=%region_37.41 | all-reduce | flops 1 | bytes 8 | tf_op jit(solution)/shard_map/psum | solution.py:17
  835.9 31.0 %psum.158 = f32[8,9]{0,1:T(8,128)S(1)} all-reduce(f32[8,9]{0,1:T(8,128)S(1)} %pad_maximum_fusion.18), channel_id=1, replica_groups=mesh['fx'=16,'fy'=8] {'fx'}, use_global_device_ids=true, to_apply=%region_38.42 | all-reduce | flops 72 | bytes 576 | tf_op jit(solution)/shard_map/psum | solution.py:18
  867.0 19.6 %psum.159 = f32[8,9]{0,1:T(8,128)S(1)} all-reduce(f32[8,9]{0,1:T(8,128)S(1)} %psum.158), channel_id=1, replica_groups=mesh['fx'=16,'fy'=8] {'fy'}, use_global_device_ids=true, to_apply=%region_39.43 | all-reduce | flops 72 | bytes 576 | tf_op jit(solution)/shard_map/psum | solution.py:17
  (431 shorter events, 312.8 us)
Async XLA Ops:
  3.3 248.6 %copy-start.26 = (s32[128]{0:T(128)}, s32[128]{0:T(128)S(1)}, u32[]{:S(2)}) copy-start(s32[128]{0:T(128)S(1)} %fusion.166) | copy-start | bytes 1540
  6.5 38.6 %all-to-all-start = ((s32[128,2,2]{1,2,0:T(2,128)}), s32[128,2,2]{1,2,0:T(2,128)S(1)}, u32[]{:S(2)}, u32[]{:S(2)}) async-start(s32[128,2,2]{1,2,0:T(2,128)} %copy.261), calls=%async_computation | async-start | bytes 262144 | tf_op jit(solution)/shard_map/all_to_all | solution.py:138
  19.6 43.1 %collective-permute-start.1 = (f32[5,8,1,128]{3,1,2,0:T(8,128)}, f32[5,8,1,128]{3,1,2,0:T(8,128)S(1)}, u32[]{:S(2)}, u32[]{:S(2)}) collective-permute-start(f32[5,8,1,128]{3,1,2,0:T(8,128)} %bitcast.176), channel_id=1, source_target_pairs={{8,0},{16,8},{24,16},{32,24},{40,32},{48,40},{56,48},{64,56},{72,6... | collective-permute-start | bytes 61448 | tf_op jit(solution)/shard_map/ppermute | solution.py:31
  25.0 37.7 %collective-permute-start = (f32[5,8,1,128]{3,1,2,0:T(8,128)}, f32[5,8,1,128]{3,1,2,0:T(8,128)S(1)}, u32[]{:S(2)}, u32[]{:S(2)}) collective-permute-start(f32[5,8,1,128]{3,1,2,0:T(8,128)} %bitcast.175), channel_id=1, source_target_pairs={{0,8},{8,16},{16,24},{24,32},{32,40},{40,48},{48,56},{56,64},{64,7... | collective-permute-start | bytes 61448 | tf_op jit(solution)/shard_map/ppermute | solution.py:29
  27.7 278.8 %collective-permute-start.5 = (f32[8,3,128]{2,0,1:T(8,128)}, f32[8,3,128]{2,0,1:T(8,128)}, u32[]{:S(2)}, u32[]{:S(2)}) collective-permute-start(f32[8,3,128]{2,0,1:T(8,128)} %convolution_bitcast_fusion.22), channel_id=1, source_target_pairs={{1,0},{2,1},{3,2},{4,3},{5,4},{6,5},{7,6},{8,7},{9,8},{10,9},{11,1... | collective-permute-start | bytes 36872 | tf_op jit(solution)/shard_map/ppermute | solution.py:31
  28.3 245.5 %collective-permute-start.4 = (f32[8,3,128]{2,1,0:T(4,128)S(1)}, f32[8,3,128]{2,1,0:T(4,128)S(1)}, u32[]{:S(2)}, u32[]{:S(2)}) collective-permute-start(f32[8,3,128]{2,1,0:T(4,128)S(1)} %copy.275), channel_id=1, source_target_pairs={{0,1},{1,2},{2,3},{3,4},{4,5},{5,6},{6,7},{7,8},{8,9},{9,10},{10,1... | collective-permute-start | bytes 36872 | tf_op jit(solution)/shard_map/ppermute | solution.py:29
  45.0 65.5 %all-to-all-start.1 = ((f32[256,3,128]{2,1,0:T(4,128)}), f32[256,3,128]{2,1,0:T(4,128)}, u32[]{:S(2)}, u32[]{:S(2)}) async-start(f32[256,3,128]{2,1,0:T(4,128)} %scatter_fusion), calls=%async_computation.1 | async-start | bytes 1048576 | tf_op jit(solution)/shard_map/all_to_all | solution.py:137
  73.4 13.5 %collective-permute-start.2 = (f32[5,8,130,1]{2,1,3,0:T(8,128)S(1)}, f32[5,8,130,1]{2,1,3,0:T(8,128)}, u32[]{:S(2)}, u32[]{:S(2)}) collective-permute-start(f32[5,8,130,1]{2,1,3,0:T(8,128)S(1)} %copy.253), channel_id=1, source_target_pairs={{0,1},{1,2},{2,3},{3,4},{4,5},{5,6},{6,7},{7,0},{8,9},{9,10},{10,1... | collective-permute-start | bytes 62408 | tf_op jit(solution)/shard_map/ppermute | solution.py:29
  78.9 11.2 %collective-permute-start.3 = (f32[5,8,130,1]{2,1,3,0:T(8,128)}, f32[5,8,130,1]{2,1,3,0:T(8,128)}, u32[]{:S(2)}, u32[]{:S(2)}) collective-permute-start(f32[5,8,130,1]{2,1,3,0:T(8,128)} %copy.254), channel_id=1, source_target_pairs={{1,0},{2,1},{3,2},{4,3},{5,4},{6,5},{7,6},{0,7},{9,8},{10,9},{11,1... | collective-permute-start | bytes 62408 | tf_op jit(solution)/shard_map/ppermute | solution.py:31
  213.7 23.2 %all-to-all-start.2 = ((f32[256,3,128]{2,1,0:T(4,128)}), f32[256,3,128]{2,1,0:T(4,128)}, u32[]{:S(2)}, u32[]{:S(2)}) async-start(f32[256,3,128]{2,1,0:T(4,128)} %convolution_bitcast_fusion.3), calls=%async_computation.2 | async-start | bytes 1048576 | tf_op jit(solution)/shard_map/all_to_all | solution.py:144
  264.3 22.6 %all-to-all-start.3 = ((f32[256,3,128]{2,1,0:T(4,128)}), f32[256,3,128]{2,1,0:T(4,128)S(1)}, u32[]{:S(2)}, u32[]{:S(2)}) async-start(f32[256,3,128]{2,1,0:T(4,128)} %scatter_fusion.1), calls=%async_computation.3 | async-start | bytes 1048576 | tf_op jit(solution)/shard_map/all_to_all | solution.py:144
  307.7 2.5 collective-permute-start.6
  310.2 3.1 collective-permute-start.7
  312.6 227.6 %copy-start.17 = (f32[8,8,3,128]{3,1,2,0:T(8,128)S(1)}, f32[8,8,3,128]{3,1,2,0:T(8,128)}, u32[]{:S(2)}) copy-start(f32[8,8,3,128]{3,1,2,0:T(8,128)} %param.52) | copy-start | bytes 294916
  423.5 2.2 collective-permute-start.8
  424.9 3.3 collective-permute-start.9
  574.3 18.0 %all-to-all-start.4 = ((f32[256,3,128]{2,1,0:T(4,128)}), f32[256,3,128]{2,1,0:T(4,128)S(1)}, u32[]{:S(2)}, u32[]{:S(2)}) async-start(f32[256,3,128]{2,1,0:T(4,128)} %convolution_bitcast_fusion.2), calls=%async_computation.4 | async-start | bytes 1048576 | tf_op jit(solution)/shard_map/all_to_all | solution.py:144
  578.4 47.9 %collective-permute-start.10 = (f32[8,3,128]{2,0,1:T(8,128)S(1)}, f32[8,3,128]{2,0,1:T(8,128)S(1)}, u32[]{:S(2)}, u32[]{:S(2)}) collective-permute-start(f32[8,3,128]{2,0,1:T(8,128)S(1)} %bitcast_subtract_fusion.1), channel_id=1, source_target_pairs={{0,1},{1,2},{2,3},{3,4},{4,5},{5,6},{6,7},{7,8},{8,9},{9,10},{10,1... | collective-permute-start | bytes 36872 | tf_op jit(solution)/shard_map/ppermute | solution.py:29
  619.1 18.0 %all-to-all-start.5 = ((f32[256,3,128]{2,1,0:T(4,128)}), f32[256,3,128]{2,1,0:T(4,128)S(1)}, u32[]{:S(2)}, u32[]{:S(2)}) async-start(f32[256,3,128]{2,1,0:T(4,128)} %scatter_fusion.2), calls=%async_computation.5 | async-start | bytes 1048576 | tf_op jit(solution)/shard_map/all_to_all | solution.py:144
  624.9 31.9 %collective-permute-start.11 = (f32[8,3,128]{2,0,1:T(8,128)S(1)}, f32[8,3,128]{2,0,1:T(8,128)S(1)}, u32[]{:S(2)}, u32[]{:S(2)}) collective-permute-start(f32[8,3,128]{2,0,1:T(8,128)S(1)} %convolution_bitcast_fusion.18), channel_id=1, source_target_pairs={{1,0},{2,1},{3,2},{4,3},{5,4},{6,5},{7,6},{8,7},{9,8},{10,9},{11,1... | collective-permute-start | bytes 36872 | tf_op jit(solution)/shard_map/ppermute | solution.py:31
  657.2 2.5 collective-permute-start.12
  659.7 3.1 collective-permute-start.13
  772.8 2.3 collective-permute-start.14
  774.2 3.4 collective-permute-start.15
  (31 other events, 1073.9 us)
